TPU v7x, 256 devices: a whole 4x4x8 slice. The times are simulated.
256 devices in a mesh: il: 16 (over y, x), xl: 16 (over z, core).
Axes of the slice: x: 4, y: 4, z: 8, core: 2. Of those that a mesh axis runs over, the one named last changes fastest.
Arguments:
- patches: bfloat16 [16, 192, 128, 768], P('il', 'xl'), may hold values from -9 to 9
- out_cot: bfloat16 [16, 192, 128, 768], P('il', 'xl'), may hold values from -6 to 6
- vis_count: int32 [16, 192], P('il', 'xl'), may hold values from 0 to 128, as said below
- w_qkv: bfloat16 [768, 1152], P(('il', 'xl')), may hold values from -1.5 to 1.5
- w_out: bfloat16 [768, 384], P(('il', 'xl')), may hold values from -0.3125 to 0.3125
- ln_gain: float32 [768], replicated, may hold values from 0.1 to 1.9
Outputs:
- enc_out: bfloat16 [16, 192, 128, 768], P('il', 'xl')
- grad_in: bfloat16 [16, 192, 128, 768], P('il', 'xl')
- grad_wqkv: float32 [768, 1152], P(('il', 'xl'))
- grad_wout: float32 [768, 384], P(('il', 'xl'))
Inputs may be any that keep to these rules, and one draw needn't show every extreme that they name: `vis_count`: A block with count 0 holds no data. On each inline row of tiles exactly 96 blocks have data; one device holds 0 to 12 of them, and some device of each row holds 12.
All inputs are finite; a program needn't handle non-finite values.
Results may differ from a plain program's by a relative error of at most 0.0096.
Values may be sent and summed in bfloat16 or wider, within the bound.
No kernel may reach another device: no remote copies, remote signals or barrier semaphores. Data moves between devices by JAX's collectives and lax.ppermute only.
A program may use at most 128 MiB of HBM per device.

v0:
```python
import jax
import jax.numpy as jnp
from jax import lax
from jax.sharding import PartitionSpec as P

HEAD_DIM = 64
HEADS = 6


def block_pass(tiles, cotan, counts, weights_qkv, weights_out, ln_gain):
    nblock, vrows, width = tiles.shape
    inner = HEADS * HEAD_DIM
    factor = HEAD_DIM ** (-0.5)
    positions = jnp.arange(vrows)
    row_mask = (positions[None, :] < counts[:, None]).astype(jnp.float32)
    tiles_f = tiles.astype(jnp.float32)
    centred = tiles_f - jnp.mean(tiles_f, axis=-1, keepdims=True)
    inv_std = lax.rsqrt(jnp.mean(centred * centred, axis=-1, keepdims=True) + 1e-06)
    normed = centred * inv_std
    normed_b = (normed * ln_gain).astype(jnp.bfloat16).reshape(nblock * vrows, width)
    project = jnp.dot(normed_b, weights_qkv, preferred_element_type=jnp.float32).astype(
        jnp.bfloat16
    )
    project = project.reshape(nblock, vrows, 3, HEADS, HEAD_DIM)
    queries = project[:, :, 0]
    keys_b = project[:, :, 1]
    values_b = project[:, :, 2]
    scores = (
        jnp.einsum("nqhe,nkhe->nhqk", queries, keys_b, preferred_element_type=jnp.float32) * factor
    )
    key_mask = (positions[None, :] < counts[:, None])[:, None, None, :]
    scores = jnp.where(key_mask, scores, jnp.float32(-1e30))
    probs_f = jnp.exp(scores - jnp.max(scores, axis=-1, keepdims=True))
    probs_f = probs_f / jnp.sum(probs_f, axis=-1, keepdims=True)
    probs_b = probs_f.astype(jnp.bfloat16)
    attended = jnp.einsum("nhqk,nkhe->nqhe", probs_b, values_b, preferred_element_type=jnp.float32)
    attended = attended.astype(jnp.bfloat16).reshape(nblock * vrows, inner)
    mixed = lax.dot_general(
        attended, weights_out, (((1,), (1,)), ((), ())), preferred_element_type=jnp.float32
    )
    mixed = mixed.reshape(nblock, vrows, width)
    encoded = ((tiles_f + mixed) * row_mask[..., None]).astype(jnp.bfloat16)
    grad_out = (cotan * row_mask[..., None].astype(jnp.bfloat16)).reshape(nblock * vrows, width)
    grad_wout = lax.dot_general(
        grad_out, attended, (((0,), (0,)), ((), ())), preferred_element_type=jnp.float32
    )
    grad_att = jnp.dot(grad_out, weights_out, preferred_element_type=jnp.float32).astype(
        jnp.bfloat16
    )
    grad_att = grad_att.reshape(nblock, vrows, HEADS, HEAD_DIM)
    grad_prob = jnp.einsum(
        "nqhe,nkhe->nhqk", grad_att, values_b, preferred_element_type=jnp.float32
    )
    grad_val = jnp.einsum("nhqk,nqhe->nkhe", probs_b, grad_att, preferred_element_type=jnp.float32)
    grad_score = (
        probs_f * (grad_prob - jnp.sum(probs_f * grad_prob, axis=-1, keepdims=True)) * factor
    )
    grad_score = grad_score.astype(jnp.bfloat16)
    grad_query = jnp.einsum(
        "nhqk,nkhe->nqhe", grad_score, keys_b, preferred_element_type=jnp.float32
    )
    grad_key = jnp.einsum(
        "nhqk,nqhe->nkhe", grad_score, queries, preferred_element_type=jnp.float32
    )
    grad_proj = (
        jnp.stack([grad_query, grad_key, grad_val], axis=2)
        .astype(jnp.bfloat16)
        .reshape(nblock * vrows, 3 * inner)
    )
    grad_wqkv = lax.dot_general(
        normed_b, grad_proj, (((0,), (0,)), ((), ())), preferred_element_type=jnp.float32
    )
    grad_norm = lax.dot_general(
        grad_proj, weights_qkv, (((1,), (1,)), ((), ())), preferred_element_type=jnp.float32
    )
    grad_norm = grad_norm.reshape(nblock, vrows, width) * ln_gain
    grad_ln = inv_std * (
        grad_norm
        - jnp.mean(grad_norm, axis=-1, keepdims=True)
        - normed * jnp.mean(grad_norm * normed, axis=-1, keepdims=True)
    )
    grad_rows = grad_out.reshape(nblock, vrows, width).astype(jnp.float32)
    grad_input = ((grad_rows + grad_ln) * row_mask[..., None]).astype(jnp.bfloat16)
    return (encoded, grad_input, grad_wqkv, grad_wout)


def shards(patches, out_cot, vis_count, w_qkv, w_out, ln_gain):
    full_qkv, full_out = (
        lax.all_gather(w_qkv, ("il", "xl"), axis=0, tiled=True),
        lax.all_gather(w_out, ("il", "xl"), axis=0, tiled=True),
    )
    tiles = patches[0]
    cotan = out_cot[0]
    counts = vis_count[0]
    encoded, grad_input, grad_qkv, grad_proj_out = block_pass(
        tiles, cotan, counts, full_qkv, full_out, ln_gain
    )
    grad_terms = jnp.concatenate([grad_qkv, grad_proj_out], axis=1)
    summed = lax.psum_scatter(grad_terms, ("il", "xl"), scatter_dimension=0, tiled=True)
    qkv_width = grad_qkv.shape[1]
    return (encoded[None], grad_input[None], summed[:, :qkv_width], summed[:, qkv_width:])


def solution(mesh):
    return jax.shard_map(
        shards,
        mesh=mesh,
        in_specs=(
            P("il", "xl", None, None),
            P("il", "xl", None, None),
            P("il", "xl"),
            P(("il", "xl"), None),
            P(("il", "xl"), None),
            P(),
        ),
        out_specs=(
            P("il", "xl", None, None),
            P("il", "xl", None, None),
            P(("il", "xl"), None),
            P(("il", "xl"), None),
        ),
        check_vma=False,
    )
```

profile of v0, /device:TPU:2, one launch (start us, length us, event | category | flops | bytes accessed | tf_op | source)
XLA Modules:
  0.0 488.9 jit_solution(13470428343686679741)
XLA Ops:
  7.2 0.0 all-gather.4.cloned.1.call-start
  7.2 0.7 all-gather.4.cloned.1.call-update
  7.9 0.0 all-reduce.3.cloned.1.call-start
  7.9 77.2 %all-gather.1 = bf16[256,3,384]{2,1,0:T(4,128)(2,1)S(1)} all-gather(bf16[1,3,384]{2,1,0:T(4,128)(2,1)} %bitcast.129), channel_id=1, replica_groups=mesh['il'=16,'xl'=16] {'il','xl'}, dimensions={0}, use_global_device_ids=true | all-gather | bytes 592128 | tf_op jit(solution)/shard_map/all_gather | solution.py:90
  85.2 1.2 reshape.185
  86.4 0.8 convert_convert_fusion
  87.2 1.9 bitcast_multiply_fusion
  89.1 0.0 copy-done.12
  89.1 2.4 convolution_convert_fusion.1
  91.6 4.8 reshape.191
  96.4 4.2 copy.45
  100.6 0.0 copy-done
  100.6 0.4 convert_reduce_fusion
  101.0 0.0 copy-start.13
  101.0 0.8 fusion.15
  101.8 0.4 copy-done.2
  102.3 1.7 broadcast_multiply_fusion
  104.0 0.0 copy-done.13
  104.0 1.9 fusion.18
  105.9 2.0 fusion.4
  107.9 11.0 %all-gather.4.cloned.1.call-done = bf16[256,3,1152]{2,1,0:T(4,128)(2,1)} async-done(((bf16[1,3,1152]{2,1,0:T(4,128)(2,1)}), bf16[256,3,1152]{2,1,0:T(4,128)(2,1)}) %all-gather.4.cloned.1.call-update) | async-done | bytes 1769488 | tf_op jit(solution)/shard_map/all_gather | solution.py:89
  118.8 5.2 %reshape.183 = bf16[768,1152]{1,0:T(8,128)(2,1)} reshape(bf16[256,3,1152]{2,1,0:T(4,128)(2,1)} %all-gather.4.cloned.1.call-done) | data formatting | bytes 3538944
  124.0 7.2 %convolution_convert_fusion = bf16[1536,1152]{1,0:T(8,128)(2,1)} fusion(bf16[1536,768]{1,0:T(8,128)(2,1)} %fusion.4, bf16[768,1152]{1,0:T(8,128)(2,1)} %reshape.183), kind=kOutput, calls=%fused_computation.2 | convolution fusion | flops 2719678464 | bytes 7667712 | tf_op jit(solution)/shard_map/dot_general | solution.py:21
  131.2 11.5 %reshape.190 = bf16[12,128,3,6,64]{4,3,2,1,0:T(8,128)(2,1)} reshape(bf16[1536,1152]{1,0:T(8,128)(2,1)} %convolution_convert_fusion) | data formatting | bytes 7077888 | tf_op jit(solution)/shard_map/reshape | solution.py:24
  142.7 6.5 %fusion.70 = (bf16[12,128,1,6,64]{4,3,2,1,0:T(8,128)(2,1)}, bf16[12,128,1,6,64]{4,3,2,1,0:T(8,128)(2,1)}, bf16[12,128,1,6,64]{4,3,2,1,0:T(8,128)(2,1)}) fusion(bf16[12,128,3,6,64]{4,3,2,1,0:T(8,128)(2,1)} %reshape.190), kind=kLoop, calls=%fused_computation.87 | loop fusion | bytes 7077888 | tf_op jit(solution)/shard_map/slice | solution.py:25
  149.2 4.2 copy.66
  153.4 4.2 copy.68
  157.7 4.2 copy.67
  161.9 2.5 fusion.51
  164.4 0.0 copy-start.5
  164.4 2.7 fusion.71
  167.1 0.0 copy-start.14
  167.2 0.0 copy-done.5
  167.2 0.0 copy-start.4
  167.2 1.8 convolution_convert_fusion.2
  169.0 0.7 copy-done.14
  169.6 0.0 copy-done.4
  169.6 2.8 convolution_bitcast_fusion
  172.4 3.0 fusion.55
  175.4 9.3 %fusion.44 = bf16[12,128,1,6,64]{1,4,3,0,2:T(8,128)(2,1)} fusion(f32[12,6,128,128]{2,3,1,0:T(8,128)} %fusion.55, bf16[12,128,1,6,64]{1,4,3,0,2:T(8,128)(2,1)} %copy.67, f32[12,6,128,128]{2,3,1,0:T(8,128)} %copy-done.14, f32[12,6,128]{2,1,0:T(8,128)S(1)} %get-tuple-element.17), kind=kOutput, calls=%fused_computation.53 | convolution fusion | flops 159261824 | bytes 11833344 | tf_op jit(solution)/shard_map/nhqk,nqhe->nkhe/dot_general | solution.py:62
  184.7 9.4 %fusion.41 = bf16[12,128,1,6,64]{1,4,3,0,2:T(8,128)(2,1)} fusion(f32[12,6,128,128]{2,3,1,0:T(8,128)} %fusion.55, bf16[12,128,1,6,64]{1,4,3,0,2:T(8,128)(2,1)} %copy.68, f32[12,6,128,128]{2,3,1,0:T(8,128)} %copy-done.14, f32[12,6,128]{2,1,0:T(8,128)S(1)} %get-tuple-element.17), kind=kOutput, calls=%fused_computation.52 | convolution fusion | flops 159261824 | bytes 11833344 | tf_op jit(solution)/shard_map/nhqk,nkhe->nqhe/dot_general | solution.py:59
  194.1 2.2 copy.53
  196.3 0.0 copy-done.8
  196.3 0.0 copy-done.9
  196.3 1.7 maximum_convert_fusion
  198.0 0.0 copy-start.7
  198.0 3.1 copy.52
  201.2 1.4 fusion.47
  202.6 0.2 copy-done.6
  202.8 3.3 fusion.23
  206.1 2.8 pad_maximum_fusion
  208.9 0.0 all-reduce.3.cloned.1.call-update
  208.9 1.2 reshape.186
  210.2 5.1 %copy.50 = bf16[12,128,3,6,64]{1,4,3,2,0:T(8,128)(2,1)} copy(bf16[12,128,3,6,64]{1,4,3,0,2:T(8,128)(2,1)} %copy-done.1) | data formatting | bytes 7077888 | tf_op jit(solution)/shard_map/convert_element_type | solution.py:67
  215.2 5.2 %reshape.187 = bf16[768,1152,1]{1,0,2:T(8,128)(2,1)} reshape(bf16[256,3,1152]{2,1,0:T(4,128)(2,1)} %all-gather.4.cloned.1.call-done) | data formatting | bytes 3538944
  220.4 6.9 %multiply_reduce_fusion.1 = (f32[12,128]{1,0:T(8,128)S(1)}, f32[12,128]{1,0:T(8,128)S(1)}, f32[12,128,768]{2,1,0:T(8,128)S(1)}) fusion(f32[768]{0:T(1024)S(1)} %copy-done.13, f32[12,128]{1,0:T(8,128)S(1)} %get-tuple-element.9, f32[12,128]{1,0:T(8,128)S(1)} %get-tuple-element.12, bf16[1,12,128,768]{3,2,1,0:T(8,128)(2,1)S(1)} %copy-done, ...), kind=kOutput, calls=%fused_computation.34 | convolution fusion | flops 2726163456 | bytes 12413952 | tf_op jit(solution)/shard_map/dot_general | solution.py:73
  227.4 0.0 copy-start.3
  227.4 0.0 copy-done.10
  227.4 0.0 copy-done.11
  227.4 3.0 fusion.34
  230.4 3.4 fusion.39
  233.8 245.4 %all-reduce.3.cloned.1.call-done = f32[768,1536]{1,0:T(8,128)} async-done(((f32[768,1536]{1,0:T(8,128)}), f32[768,1536]{1,0:T(8,128)}) %all-reduce.3.cloned.1.call-update) | async-done | bytes 4718608
  479.2 1.5 constant_dynamic-slice_fusion
  480.7 1.4 dynamic-slice.2
  (15 shorter events, 0.0 us)
Async XLA Ops:
  7.2 111.6 %all-gather.4.cloned.1.call-start = ((), (), s32[]{:S(2)}) async-start(), calls=%async_computation | async-start | bytes 2368512 | tf_op jit(solution)/shard_map/all_gather | solution.py:89
  7.9 471.3 %all-reduce.3.cloned.1.call-start = ((), (), s32[]{:S(2)}) async-start(), calls=%async_computation.1 | async-start | bytes 9437184
  86.4 2.7 copy-start.12
  91.6 9.0 %copy-start = (bf16[1,12,128,768]{3,2,1,0:T(8,128)(2,1)S(1)}, bf16[1,12,128,768]{3,2,1,0:T(8,128)(2,1)}, u32[]{:S(2)}) copy-start(bf16[1,12,128,768]{3,2,1,0:T(8,128)(2,1)} %param.6) | copy-start | bytes 7077892
  100.6 1.7 copy-start.2
  101.0 3.0 copy-start.13
  164.4 2.8 copy-start.5
  167.1 2.5 copy-start.14
  167.2 2.5 copy-start.4
  194.0 2.2 copy-start.8
  194.1 2.3 copy-start.9
  198.0 3.1 copy-start.1
  198.0 3.1 copy-start.7
  201.2 1.7 copy-start.6
  220.4 7.0 %copy-start.10 = (bf16[12,6,64,128]{3,2,1,0:T(8,128)(2,1)S(1)}, bf16[12,6,64,128]{3,2,1,0:T(8,128)(2,1)}, u32[]{:S(2)}) copy-start(bf16[12,6,64,128]{3,2,1,0:T(8,128)(2,1)} %convolution_convert_fusion.2) | copy-start | bytes 3538948
  220.4 7.0 %copy-start.11 = (bf16[768,384,1]{1,0,2:T(8,128)(2,1)S(1)}, bf16[768,384,1]{1,0,2:T(8,128)(2,1)}, u32[]{:S(2)}) copy-start(bf16[768,384,1]{1,0,2:T(8,128)(2,1)} %reshape.186) | copy-start | bytes 1769476
  227.4 3.0 copy-start.3
Sparse Core Ops, SparseCore 0:
  11.6 107.2 all-gather.3
  209.0 270.0 all-reduce.2
where the time goes:
time: 490 us; the launch traced here: 489 us
  waiting for transfers between devices  257 us (52%)
  blocking collectives  77.2 us (16%)
  local copies, waits for them, and re-layouts  67.3 us (14%)
  matrix products  52.9 us (11%)
  other arithmetic  20.1 us (4%)
  between operations  14.3 us (3%)
    unnamed x3, waiting for transfers between devices  246 us
    all_gather x1, blocking collectives, shards(): lax.all_gather(w_out, ('il', 'xl'), axis=0, tiled=True)  77.2 us
    unnamed x37, local copies, waits for them, and re-layouts  27 us
    reshape x1, local copies, waits for them, and re-layouts, block_pass(): project = project.reshape(nblock, vrows, 3, HEADS, HEAD_DIM)  11.5 us
    all_gather x1, waiting for transfers between devices, shards(): lax.all_gather(w_qkv, ('il', 'xl'), axis=0, tiled=True)  11 us
  transfers between devices with their start and end apart: 2, of which 2 were waited for; matrix products, arithmetic and copies ran while one was open for 10% of the time, Pallas kernels for 0%

commit v1 on v0

--- a/solution.py
+++ b/solution.py
@@ -87,7 +87,10 @@
 def shards(patches, out_cot, vis_count, w_qkv, w_out, ln_gain):
     full_qkv, full_out = (
         lax.all_gather(w_qkv, ("il", "xl"), axis=0, tiled=True),
-        lax.all_gather(w_out, ("il", "xl"), axis=0, tiled=True),
+        jnp.concatenate(
+            lax.all_to_all(jnp.stack([w_out] * lax.axis_size(("il", "xl"))), ("il", "xl"), 0, 0),
+            axis=0,
+        ),
     )
     tiles = patches[0]
     cotan = out_cot[0]

time: 490 us -> 492 us (level)
  blocking collectives: 77.2 us -> 0 us
  waiting for transfers between devices: 257 us -> 320 us
  starting transfers between devices: 0.08 us -> 14.8 us
    all_gather x1 -> x0, blocking collectives: 77.2 us -> none  [shards(): lax.all_gather(w_out, ('il', 'xl'), axis=0, tiled=True)]
    all_gather x1, waiting for transfers between devices: 11 us -> 56 us  [shards(): lax.all_gather(w_qkv, ('il', 'xl'), axis=0, tiled=True)]
    all_to_all x0 -> x1, waiting for transfers between devices: none -> 17.5 us  [shards(): lax.all_to_all(jnp.stack([w_out] * lax.axis_size(('il', 'xl'))), ('il', '...]
    all_to_all x0 -> x1, starting transfers between devices: none -> 14.7 us  [shards(): lax.all_to_all(jnp.stack([w_out] * lax.axis_size(('il', 'xl'))), ('il', '...]
    unnamed x37 -> x33, local copies, waits for them, and re-layouts: 27 us -> 23.9 us
  transfers between devices with their start and end apart: 2 -> 3, of which waited for: 2 -> 3; matrix products, arithmetic and copies ran while one was open for 10% -> 10% of each run, Pallas kernels for 0% -> 0%
where the time goes in v1:
time: 492 us; the launch traced here: 491 us
  waiting for transfers between devices  320 us (65%)
  local copies, waits for them, and re-layouts  68.1 us (14%)
  matrix products  56.3 us (11%)
  other arithmetic  17.3 us (4%)
  starting transfers between devices  14.8 us (3%)
  between operations  14.3 us (3%)
    unnamed x3, waiting for transfers between devices  246 us
    all_gather x1, waiting for transfers between devices, shards(): lax.all_gather(w_qkv, ('il', 'xl'), axis=0, tiled=True)  56 us
    unnamed x33, local copies, waits for them, and re-layouts  23.9 us
    all_to_all x1, waiting for transfers between devices, shards(): lax.all_to_all(jnp.stack([w_out] * lax.axis_size(('il', 'xl'))), ('il', '...  17.5 us
    all_to_all x1, starting transfers between devices, shards(): lax.all_to_all(jnp.stack([w_out] * lax.axis_size(('il', 'xl'))), ('il', '...  14.7 us
    reshape x1, local copies, waits for them, and re-layouts, block_pass(): project = project.reshape(nblock, vrows, 3, HEADS, HEAD_DIM)  11.5 us
  transfers between devices with their start and end apart: 3, of which 3 were waited for; matrix products, arithmetic and copies ran while one was open for 10% of the time, Pallas kernels for 0%

profile of v1, /device:TPU:2, one launch (start us, length us, event | category | flops | bytes accessed | tf_op | source)
XLA Modules:
  0.0 490.6 jit_solution(8502589810454640752)
XLA Ops:
  7.2 0.0 copy-start
  7.2 0.0 all-gather.3.cloned.1.call-start
  7.2 0.7 all-gather.3.cloned.1.call-update
  7.9 1.8 stack.10
  9.7 14.7 %all-to-all-start = ((bf16[256,3,384]{2,1,0:T(4,128)(2,1)}), bf16[256,3,384]{2,1,0:T(4,128)(2,1)S(1)}, u32[]{:S(2)}, u32[]{:S(2)}) async-start(bf16[256,3,384]{2,1,0:T(4,128)(2,1)} %stack.10), calls=%async_computation | async-start | bytes 1572864 | tf_op jit(solution)/shard_map/all_to_all | solution.py:91
  24.4 0.0 all-reduce.3.cloned.1.call-start
  24.4 0.0 copy-start.2
  24.4 0.9 convert_convert_fusion
  25.3 0.0 copy-done
  25.3 0.4 convert_reduce_fusion
  25.7 0.0 copy-start.12
  25.7 0.8 fusion.15
  26.6 0.0 copy-done.2
  26.6 1.7 broadcast_multiply_fusion
  28.3 0.0 copy-done.12
  28.3 1.9 fusion.18
  30.2 2.0 fusion.4
  32.2 17.5 %all-to-all-done = bf16[256,3,384]{2,1,0:T(4,128)(2,1)S(1)} async-done(((bf16[256,3,384]{2,1,0:T(4,128)(2,1)}), bf16[256,3,384]{2,1,0:T(4,128)(2,1)S(1)}, u32[]{:S(2)}, u32[]{:S(2)}) %all-to-all-start) | async-done | bytes 589856 | tf_op jit(solution)/shard_map/all_to_all | solution.py:91
  49.7 1.2 reshape.187
  50.9 4.2 convolution_convert_fusion.1
  55.1 4.7 reshape.198
  59.8 4.2 copy.45
  64.0 56.0 %all-gather.3.cloned.1.call-done = bf16[256,3,1152]{2,1,0:T(4,128)(2,1)} async-done(((bf16[1,3,1152]{2,1,0:T(4,128)(2,1)}), bf16[256,3,1152]{2,1,0:T(4,128)(2,1)}) %all-gather.3.cloned.1.call-update) | async-done | bytes 1769488 | tf_op jit(solution)/shard_map/all_gather | solution.py:89
  120.0 5.2 %reshape.192 = bf16[768,1152]{1,0:T(8,128)(2,1)} reshape(bf16[256,3,1152]{2,1,0:T(4,128)(2,1)} %all-gather.3.cloned.1.call-done) | data formatting | bytes 3538944
  125.2 7.2 %convolution_convert_fusion = bf16[1536,1152]{1,0:T(8,128)(2,1)} fusion(bf16[1536,768]{1,0:T(8,128)(2,1)} %fusion.4, bf16[768,1152]{1,0:T(8,128)(2,1)} %reshape.192), kind=kOutput, calls=%fused_computation.2 | convolution fusion | flops 2719678464 | bytes 7667712 | tf_op jit(solution)/shard_map/dot_general | solution.py:21
  132.4 11.5 %reshape.197 = bf16[12,128,3,6,64]{4,3,2,1,0:T(8,128)(2,1)} reshape(bf16[1536,1152]{1,0:T(8,128)(2,1)} %convolution_convert_fusion) | data formatting | bytes 7077888 | tf_op jit(solution)/shard_map/reshape | solution.py:24
  143.9 6.5 %fusion.69 = (bf16[12,128,1,6,64]{4,3,2,1,0:T(8,128)(2,1)}, bf16[12,128,1,6,64]{4,3,2,1,0:T(8,128)(2,1)}, bf16[12,128,1,6,64]{4,3,2,1,0:T(8,128)(2,1)}) fusion(bf16[12,128,3,6,64]{4,3,2,1,0:T(8,128)(2,1)} %reshape.197), kind=kLoop, calls=%fused_computation.85 | loop fusion | bytes 7077888 | tf_op jit(solution)/shard_map/slice | solution.py:25
  150.4 4.2 copy.66
  154.6 4.2 copy.68
  158.8 4.3 copy.67
  163.1 2.5 fusion.51
  165.6 0.0 copy-start.5
  165.6 2.7 fusion.70
  168.3 0.0 copy-start.13
  168.3 0.0 copy-done.5
  168.3 0.0 copy-start.4
  168.3 1.8 convolution_convert_fusion.2
  170.1 0.7 copy-done.13
  170.8 0.0 copy-done.4
  170.8 2.8 convolution_bitcast_fusion
  173.6 3.0 fusion.55
  176.6 9.3 %fusion.44 = bf16[12,128,1,6,64]{1,4,3,0,2:T(8,128)(2,1)} fusion(f32[12,6,128,128]{2,3,1,0:T(8,128)} %fusion.55, bf16[12,128,1,6,64]{1,4,3,0,2:T(8,128)(2,1)} %copy.67, f32[12,6,128,128]{2,3,1,0:T(8,128)} %copy-done.13, f32[12,6,128]{2,1,0:T(8,128)S(1)} %get-tuple-element.16), kind=kOutput, calls=%fused_computation.52 | convolution fusion | flops 159261824 | bytes 11833344 | tf_op jit(solution)/shard_map/nhqk,nqhe->nkhe/dot_general | solution.py:62
  185.9 9.4 %fusion.41 = bf16[12,128,1,6,64]{1,4,3,0,2:T(8,128)(2,1)} fusion(f32[12,6,128,128]{2,3,1,0:T(8,128)} %fusion.55, bf16[12,128,1,6,64]{1,4,3,0,2:T(8,128)(2,1)} %copy.68, f32[12,6,128,128]{2,3,1,0:T(8,128)} %copy-done.13, f32[12,6,128]{2,1,0:T(8,128)S(1)} %get-tuple-element.16), kind=kOutput, calls=%fused_computation.51 | convolution fusion | flops 159261824 | bytes 11833344 | tf_op jit(solution)/shard_map/nhqk,nkhe->nqhe/dot_general | solution.py:59
  195.3 2.1 copy.53
  197.4 0.0 copy-start.7
  197.4 0.0 copy-start.8
  197.4 3.2 fusion.47
  200.7 0.7 maximum_convert_fusion
  201.4 3.1 copy.52
  204.4 0.0 copy-done.1
  204.5 0.0 copy-done.6
  204.5 3.3 fusion.23
  207.7 2.8 pad_maximum_fusion
  210.5 0.0 all-reduce.3.cloned.1.call-update
  210.6 1.2 reshape.193
  211.8 5.1 %copy.50 = bf16[12,128,3,6,64]{1,4,3,2,0:T(8,128)(2,1)} copy(bf16[12,128,3,6,64]{1,4,3,0,2:T(8,128)(2,1)} %copy-done.1) | data formatting | bytes 7077888 | tf_op jit(solution)/shard_map/convert_element_type | solution.py:67
  216.9 5.2 %reshape.194 = bf16[768,1152,1]{1,0,2:T(8,128)(2,1)} reshape(bf16[256,3,1152]{2,1,0:T(4,128)(2,1)} %all-gather.3.cloned.1.call-done) | data formatting | bytes 3538944
  222.1 6.7 %multiply_reduce_fusion.1 = (f32[12,128]{1,0:T(8,128)S(1)}, f32[12,128]{1,0:T(8,128)S(1)}, f32[12,128,768]{2,1,0:T(8,128)S(1)}) fusion(f32[768]{0:T(1024)S(1)} %copy-done.12, f32[12,128]{1,0:T(8,128)S(1)} %get-tuple-element.9, f32[12,128]{1,0:T(8,128)S(1)} %get-tuple-element.12, bf16[1,12,128,768]{3,2,1,0:T(8,128)(2,1)S(1)} %copy-done, ...), kind=kOutput, calls=%fused_computation.34 | convolution fusion | flops 2726163456 | bytes 12413952 | tf_op jit(solution)/shard_map/dot_general | solution.py:73
  228.8 0.0 copy-start.3
  228.8 3.0 fusion.34
  231.8 3.4 fusion.39
  235.2 245.7 %all-reduce.3.cloned.1.call-done = f32[768,1536]{1,0:T(8,128)} async-done(((f32[768,1536]{1,0:T(8,128)}), f32[768,1536]{1,0:T(8,128)}) %all-reduce.3.cloned.1.call-update) | async-done | bytes 4718608
  480.9 1.5 constant_dynamic-slice_fusion
  482.4 1.4 dynamic-slice.2
  (14 shorter events, 0.0 us)
Async XLA Ops:
  7.2 18.2 %copy-start = (bf16[1,12,128,768]{3,2,1,0:T(8,128)(2,1)S(1)}, bf16[1,12,128,768]{3,2,1,0:T(8,128)(2,1)}, u32[]{:S(2)}) copy-start(bf16[1,12,128,768]{3,2,1,0:T(8,128)(2,1)} %param.6) | copy-start | bytes 7077892
  7.2 112.8 %all-gather.3.cloned.1.call-start = ((), (), s32[]{:S(2)}) async-start(), calls=%async_computation.1 | async-start | bytes 2368512 | tf_op jit(solution)/shard_map/all_gather | solution.py:89
  9.7 40.0 %all-to-all-start = ((bf16[256,3,384]{2,1,0:T(4,128)(2,1)}), bf16[256,3,384]{2,1,0:T(4,128)(2,1)S(1)}, u32[]{:S(2)}, u32[]{:S(2)}) async-start(bf16[256,3,384]{2,1,0:T(4,128)(2,1)} %stack.10), calls=%async_computation | async-start | bytes 1572864 | tf_op jit(solution)/shard_map/all_to_all | solution.py:91
  24.4 456.5 %all-reduce.3.cloned.1.call-start = ((), (), s32[]{:S(2)}) async-start(), calls=%async_computation.2 | async-start | bytes 9437184
  24.4 2.1 copy-start.2
  25.7 2.5 copy-start.12
  165.6 2.8 copy-start.5
  168.3 2.5 copy-start.13
  168.3 2.5 copy-start.4
  197.4 3.3 copy-start.7
  197.4 3.3 copy-start.8
  197.4 3.3 copy-start.9
  201.3 3.1 copy-start.1
  201.3 3.1 copy-start.6
  222.1 6.7 %copy-start.10 = (bf16[12,6,64,128]{3,2,1,0:T(8,128)(2,1)S(1)}, bf16[12,6,64,128]{3,2,1,0:T(8,128)(2,1)}, u32[]{:S(2)}) copy-start(bf16[12,6,64,128]{3,2,1,0:T(8,128)(2,1)} %convolution_convert_fusion.2) | copy-start | bytes 3538948
  222.1 6.7 %copy-start.11 = (bf16[768,384,1]{1,0,2:T(8,128)(2,1)S(1)}, bf16[768,384,1]{1,0,2:T(8,128)(2,1)}, u32[]{:S(2)}) copy-start(bf16[768,384,1]{1,0,2:T(8,128)(2,1)} %reshape.193) | copy-start | bytes 1769476
  228.8 3.0 copy-start.3
Sparse Core Ops, SparseCore 0:
  11.6 108.3 all-gather.2
  210.7 270.1 all-reduce.2
